TPU v7x, 32 devices: a whole 2x2x4 slice. The times are simulated.
32 devices in a mesh: mem: 4 (over x, core), tile: 8 (over z, y).
Axes of the slice: x: 2, y: 2, z: 4, core: 2. Of those that a mesh axis runs over, the one named last changes fastest.
Arguments:
- increment: float32 [70, 128, 256], P(None, 'tile')
- previous: float32 [70, 128, 256], P(None, 'tile'), may hold values from -6 to 6
- beta_prev: float32 [1], replicated, may hold values from 0.5 to 1.5
- members: bfloat16 [8, 70, 128, 256], P('mem', None, 'tile'), may hold values from -6 to 6
- band_widths: int32 [70], replicated, may hold values from 1 to 8, as said below
- diffusion_steps: int32 [8], replicated, may hold values from 1 to 4, as said below
Outputs:
- next_vector: float32 [70, 128, 256], P(None, 'tile')
- coefficients: float32 [2], replicated
Inputs may be any that keep to these rules, and one draw needn't show every extreme that they name: `band_widths`: every level's band width lies in the range and some level has exactly 8. `diffusion_steps`: every tile's iteration count lies in the range and some tile has exactly 4.
All inputs are finite; a program needn't handle non-finite values.
Results may differ from a plain program's by a relative error of at most 0.0003.
Values sent between devices are 32-bit elements; how exact they have to be, the bound alone decides.
No kernel may reach another device: no remote copies, remote signals or barrier semaphores. Data moves between devices by JAX's collectives and lax.ppermute only.
A program may use at most 64 MiB of HBM per device.

v0:
```python
import jax
import jax.numpy as jnp
from jax import lax
from jax.sharding import PartitionSpec as P

MEM_DEV = 2
DIFF = 4


def extended(value, sides, width):
    for axis, dim in sides:
        count, length = (lax.axis_size(axis), value.shape[dim])
        up = [(i, (i + 1) % count) for i in range(count - 1)]
        down = [(j, i) for i, j in up]
        last = lax.slice_in_dim(value, length - width, length, axis=dim)
        leading = lax.slice_in_dim(value, 0, width, axis=dim)
        before = lax.ppermute(last, axis, up)
        after = lax.ppermute(leading, axis, down)
        value = jnp.concatenate([before, value, after], axis=dim)
    return value


def vertical_matrix(band_widths):
    levels = jnp.arange(band_widths.shape[0], dtype=jnp.int32)
    apart = levels[:, None] - levels[None, :]
    band_float = band_widths.astype(jnp.float32)
    limit = jnp.minimum(band_widths[:, None], band_widths[None, :])
    weight = jnp.exp(-apart.astype(jnp.float32) ** 2 / (band_float[:, None] * band_float[None, :]))
    return jnp.where(jnp.abs(apart) <= limit, weight, jnp.float32(0.0))


def lanczos_sums(image_part, incr_part, prev_part, beta_value):
    inc_img, inc_inc = lax.psum(
        (jnp.sum(incr_part * image_part), jnp.sum(incr_part * incr_part)), ("mem", "tile")
    )
    alpha_value = inc_img / inc_inc
    residual = image_part - alpha_value * incr_part - beta_value * prev_part
    squares = lax.psum(jnp.sum(residual * residual), ("mem", "tile"))
    return (alpha_value, squares)


def row_owner_counts(diffusion_steps, first_row, row_total, tile_rows):
    global_rows = first_row + jnp.arange(row_total, dtype=jnp.int32)
    owner = jnp.floor_divide(global_rows, tile_rows)
    tile_ids = jnp.arange(diffusion_steps.shape[0], dtype=jnp.int32)
    matches = (owner[:, None] == tile_ids[None, :]).astype(jnp.int32)
    return jnp.sum(matches * diffusion_steps[None, :], axis=1)


def per_device(increment, previous, beta_prev, members, band_widths, diffusion_steps):
    vertical = vertical_matrix(band_widths)
    tile_rows = increment.shape[1]
    tile_here = lax.axis_index("tile")
    members_f = members.astype(jnp.float32)
    localized = jnp.einsum(
        "ij,mjyx->miyx", vertical, members_f * increment[None], precision=lax.Precision.HIGHEST
    )
    step_count = row_owner_counts(diffusion_steps, tile_here * tile_rows, tile_rows, tile_rows)[
        None, None, :, None
    ]
    for sweep_index in range(DIFF):
        padded = extended(localized, (("tile", 2),), 1)
        sideways = jnp.pad(localized, ((0, 0), (0, 0), (0, 0), (1, 1)))
        laplace = (
            padded[:, :, 2:, :]
            + padded[:, :, :-2, :]
            + sideways[:, :, :, 2:]
            + sideways[:, :, :, :-2]
            - 4.0 * localized
        )
        localized = jnp.where(sweep_index < step_count, localized + 0.24 * laplace, localized)
    partial_value = jnp.sum(members_f * localized, axis=0)
    inverse_count = 1.0 / (MEM_DEV * lax.axis_size("mem") - 1)
    beta_value = beta_prev[0]
    cells_all = increment.shape[0] * increment.shape[1] * lax.axis_size("tile") * increment.shape[2]
    share_width = increment.shape[2] // lax.axis_size("mem")
    offset = lax.axis_index("mem") * share_width
    incr_share = lax.dynamic_slice_in_dim(increment, offset, share_width, 2)
    prev_share = lax.dynamic_slice_in_dim(previous, offset, share_width, 2)
    summed = lax.psum(partial_value, "mem")
    image = increment + summed * inverse_count
    image_share = lax.dynamic_slice_in_dim(image, offset, share_width, 2)
    alpha_value, squares = lanczos_sums(image_share, incr_share, prev_share, beta_value)
    scale_value = jnp.sqrt(squares / cells_all + 1e-06)
    residual = image - alpha_value * increment - beta_value * previous
    next_vector = residual / scale_value
    coefficients = jnp.stack([alpha_value, scale_value])
    return (next_vector, coefficients)


def solution(mesh):
    in_specs = (
        P(None, "tile", None),
        P(None, "tile", None),
        P(),
        P("mem", None, "tile", None),
        P(),
        P(),
    )
    out_specs = (P(None, "tile", None), P())
    return jax.shard_map(
        per_device, mesh=mesh, in_specs=in_specs, out_specs=out_specs, check_vma=False
    )
```

profile of v0, /device:TPU:0, one launch (start us, length us, event | category | flops | bytes accessed | tf_op | source)
XLA Modules:
  0.0 210.4 jit_solution(6761432922234523690)
XLA Ops:
  7.2 2.0 copy.20
  9.9 3.4 %fusion.22 = f32[2,70,16,256]{3,1,2,0:T(8,128)S(1)} fusion(f32[70,16,256]{2,0,1:T(8,128)S(1)} %copy.20, bf16[2,70,16,256]{3,2,1,0:T(8,128)(2,1)S(1)} %copy-done.1, f32[70]{0:T(128)S(1)} %convert_element_type.17, s32[70]{0:T(128)} %param.10), kind=kOutput, calls=%fused_computation.44 | convolution fusion | flops 482885472 | bytes 4588080 | tf_op jit(solution)/shard_map/ij,mjyx->miyx/dot_general | solution.py:55
  13.3 0.7 fusion.45
  14.1 1.3 collective-permute-start
  15.4 6.2 %collective-permute-start.1 = (f32[2,70,1,256]{3,1,2,0:T(8,128)}, f32[2,70,1,256]{3,1,2,0:T(8,128)}, u32[]{:S(2)}, u32[]{:S(2)}) collective-permute-start(f32[2,70,1,256]{3,1,2,0:T(8,128)} %get-tuple-element.17), channel_id=1, source_target_pairs={{0,1},{1,2},{2,3},{3,4},{4,5},{5,6},{6,7},{8,9},{9,10},{10,11},{11... | collective-permute-start | bytes 430088 | tf_op jit(solution)/shard_map/ppermute | solution.py:17
  21.6 1.5 collective-permute-done
  23.1 3.3 %collective-permute-done.1 = f32[2,70,1,256]{3,1,2,0:T(8,128)} collective-permute-done((f32[2,70,1,256]{3,1,2,0:T(8,128)}, f32[2,70,1,256]{3,1,2,0:T(8,128)}, u32[]{:S(2)}, u32[]{:S(2)}) %collective-permute-start.1) | collective-permute-done | bytes 143392 | tf_op jit(solution)/shard_map/ppermute | solution.py:17
  26.4 2.6 %add_select_fusion.3 = f32[2,70,16,256]{3,1,2,0:T(8,128)S(1)} fusion(f32[2,70,16,256]{3,1,2,0:T(8,128)S(1)} %fusion.22, f32[2,70,1,256]{3,1,2,0:T(8,128)} %collective-permute-done.1, f32[2,70,1,256]{3,1,2,0:T(8,128)} %collective-permute-done, pred[16]{0:T(512)(128)(4,1)S(1)} %get-tuple-element.19), kind=kLoop, calls=%fused_computation.11 | loop fusion | flops 5734400 | bytes 4874256 | tf_op jit(solution)/shard_map/jit(_where)/select_n | solution.py:71
  29.1 1.3 collective-permute-start.2
  30.4 5.0 %collective-permute-start.3 = (f32[2,70,1,256]{3,1,2,0:T(8,128)S(1)}, f32[2,70,1,256]{3,1,2,0:T(8,128)S(1)}, u32[]{:S(2)}, u32[]{:S(2)}) collective-permute-start(f32[2,70,1,256]{3,1,2,0:T(8,128)S(1)} %get-tuple-element.15), channel_id=1, source_target_pairs={{0,1},{1,2},{2,3},{3,4},{4,5},{5,6},{6,7},{8,9},{9,10},{10,11},{11... | collective-permute-start | bytes 430088 | tf_op jit(solution)/shard_map/ppermute | solution.py:17
  35.4 2.1 collective-permute-done.2
  37.5 3.3 %collective-permute-done.3 = f32[2,70,1,256]{3,1,2,0:T(8,128)S(1)} collective-permute-done((f32[2,70,1,256]{3,1,2,0:T(8,128)S(1)}, f32[2,70,1,256]{3,1,2,0:T(8,128)S(1)}, u32[]{:S(2)}, u32[]{:S(2)}) %collective-permute-start.3) | collective-permute-done | bytes 143392 | tf_op jit(solution)/shard_map/ppermute | solution.py:17
  40.8 1.8 add_select_fusion.2
  42.6 1.3 collective-permute-start.4
  43.9 5.0 %collective-permute-start.5 = (f32[2,70,1,256]{3,1,2,0:T(8,128)S(1)}, f32[2,70,1,256]{3,1,2,0:T(8,128)S(1)}, u32[]{:S(2)}, u32[]{:S(2)}) collective-permute-start(f32[2,70,1,256]{3,1,2,0:T(8,128)S(1)} %get-tuple-element.13), channel_id=1, source_target_pairs={{0,1},{1,2},{2,3},{3,4},{4,5},{5,6},{6,7},{8,9},{9,10},{10,11},{11... | collective-permute-start | bytes 430088 | tf_op jit(solution)/shard_map/ppermute | solution.py:17
  48.9 2.1 collective-permute-done.4
  51.0 3.3 %collective-permute-done.5 = f32[2,70,1,256]{3,1,2,0:T(8,128)S(1)} collective-permute-done((f32[2,70,1,256]{3,1,2,0:T(8,128)S(1)}, f32[2,70,1,256]{3,1,2,0:T(8,128)S(1)}, u32[]{:S(2)}, u32[]{:S(2)}) %collective-permute-start.5) | collective-permute-done | bytes 143392 | tf_op jit(solution)/shard_map/ppermute | solution.py:17
  54.3 1.7 add_select_fusion.1
  56.1 1.3 collective-permute-start.6
  57.4 5.0 %collective-permute-start.7 = (f32[2,70,1,256]{3,1,2,0:T(8,128)S(1)}, f32[2,70,1,256]{3,1,2,0:T(8,128)S(1)}, u32[]{:S(2)}, u32[]{:S(2)}) collective-permute-start(f32[2,70,1,256]{3,1,2,0:T(8,128)S(1)} %get-tuple-element.11), channel_id=1, source_target_pairs={{0,1},{1,2},{2,3},{3,4},{4,5},{5,6},{6,7},{8,9},{9,10},{10,11},{11... | collective-permute-start | bytes 430088 | tf_op jit(solution)/shard_map/ppermute | solution.py:17
  62.4 2.1 collective-permute-done.6
  64.5 3.3 %collective-permute-done.7 = f32[2,70,1,256]{3,1,2,0:T(8,128)S(1)} collective-permute-done((f32[2,70,1,256]{3,1,2,0:T(8,128)S(1)}, f32[2,70,1,256]{3,1,2,0:T(8,128)S(1)}, u32[]{:S(2)}, u32[]{:S(2)}) %collective-permute-start.7) | collective-permute-done | bytes 143392 | tf_op jit(solution)/shard_map/ppermute | solution.py:17
  67.8 3.8 %fusion.1 = f32[70,16,256]{2,0,1:T(8,128)} fusion(f32[2,70,16,256]{3,1,2,0:T(8,128)S(1)} %add_select_fusion.1, f32[2,70,1,256]{3,1,2,0:T(8,128)S(1)} %collective-permute-done.7, f32[2,70,1,256]{3,1,2,0:T(8,128)S(1)} %collective-permute-done.6, pred[16]{0:T(512)(128)(4,1)S(1)} %get-tuple-element.18, bf16[2,70,16,256]{3,2,1,0:T(8,128)(2,1)S(1)} %copy-done.2), kind=kLoop, calls=%fused_computation.15 | loop fusion | flops 7168000 | bytes 4874256 | tf_op jit(solution)/shard_map/reduce_sum | solution.py:72
  72.4 1.7 copy.23
  74.1 36.2 %all-reduce.7.cloned.1.call-done = f32[70,16,256]{2,0,1:T(8,128)} async-done(((f32[70,16,256]{2,0,1:T(8,128)}), f32[70,16,256]{2,0,1:T(8,128)}) %all-reduce.7.cloned.1.call-update) | async-done | bytes 1146896 | tf_op jit(solution)/shard_map/psum | solution.py:80
  110.4 2.0 multiply_add_fusion
  112.4 1.0 multiply_reduce_fusion.1
  113.3 39.7 %all-reduce.4 = (f32[]{:T(128)}, f32[]{:T(128)}) all-reduce(f32[]{:T(128)} %get-tuple-element.7, f32[]{:T(128)} %get-tuple-element.6), channel_id=1, replica_groups=mesh['mem'=4,'tile'=8] {'mem','tile'}, use_global_device_ids=true, to_apply=%region_4.5 | all-reduce | flops 2 | bytes 16 | tf_op jit(solution)/shard_map/psum | solution.py:33
  154.4 2.2 %multiply_reduce_fusion = f32[]{:T(128)} fusion(f32[70,16,256]{2,0,1:T(8,128)} %copy.23, s32[]{:T(128)S(6)} %select_n.37, f32[70,16,256]{2,0,1:T(8,128)S(1)} %multiply_add_fusion, f32[70,16,256]{2,0,1:T(8,128)S(1)} %copy.20, f32[]{:T(128)} %bitcast.11, f32[]{:T(128)} %div.32), kind=kLoop, calls=%fused_computation.49 | loop fusion | flops 430079 | bytes 860176 | tf_op jit(solution)/shard_map/reduce_sum | solution.py:38
  156.6 41.4 %psum.31 = f32[]{:T(128)} all-reduce(f32[]{:T(128)} %multiply_reduce_fusion), channel_id=1, replica_groups=mesh['mem'=4,'tile'=8] {'mem','tile'}, use_global_device_ids=true, to_apply=%region_8.9 | all-reduce | flops 1 | bytes 8 | tf_op jit(solution)/shard_map/psum | solution.py:38
  198.6 3.0 %subtract_divide_fusion = f32[70,16,256]{2,0,1:T(8,128)S(1)} fusion(f32[]{:T(128)} %sqrt.3, f32[]{:T(128)} %bitcast.10, f32[]{:T(128)} %div.32, f32[70,16,256]{2,1,0:T(8,128)} %param.7, f32[70,16,256]{2,1,0:T(8,128)S(1)} %copy-done, f32[70,16,256]{2,0,1:T(8,128)} %all-reduce.7.cloned.1.call-done), kind=kLoop, calls=%fused_computation.45 | loop fusion | flops 2007040 | bytes 4587532 | tf_op jit(solution)/shard_map/div | solution.py:86
  201.6 1.4 copy.25
  (20 shorter events, 1.5 us)
Async XLA Ops:
  7.2 103.2 %all-reduce.7.cloned.1.call-start = ((), (), s32[]{:S(2)}) async-start(), calls=%async_computation | async-start | bytes 2359296 | tf_op jit(solution)/shard_map/psum | solution.py:80
  7.2 2.7 %copy-start.1 = (bf16[2,70,16,256]{3,2,1,0:T(8,128)(2,1)S(1)}, bf16[2,70,16,256]{3,2,1,0:T(8,128)(2,1)}, u32[]{:S(2)}) copy-start(bf16[2,70,16,256]{3,2,1,0:T(8,128)(2,1)} %param.9) | copy-start | bytes 3440644
  9.9 11.6 %copy-start.4 = (s32[8]{0:T(128)S(1)}, s32[8]{0:T(128)}, u32[]{:S(2)}) copy-start(s32[8]{0:T(128)} %param.11) | copy-start | bytes 100
  14.1 9.0 %collective-permute-start = (f32[2,70,1,256]{3,1,2,0:T(8,128)}, f32[2,70,1,256]{3,1,2,0:T(8,128)}, u32[]{:S(2)}, u32[]{:S(2)}) collective-permute-start(f32[2,70,1,256]{3,1,2,0:T(8,128)} %get-tuple-element.16), channel_id=1, source_target_pairs={{1,0},{2,1},{3,2},{4,3},{5,4},{6,5},{7,6},{9,8},{10,9},{11,10},{12... | collective-permute-start | bytes 430088 | tf_op jit(solution)/shard_map/ppermute | solution.py:18
  15.4 11.0 %collective-permute-start.1 = (f32[2,70,1,256]{3,1,2,0:T(8,128)}, f32[2,70,1,256]{3,1,2,0:T(8,128)}, u32[]{:S(2)}, u32[]{:S(2)}) collective-permute-start(f32[2,70,1,256]{3,1,2,0:T(8,128)} %get-tuple-element.17), channel_id=1, source_target_pairs={{0,1},{1,2},{2,3},{3,4},{4,5},{5,6},{6,7},{8,9},{9,10},{10,11},{11... | collective-permute-start | bytes 430088 | tf_op jit(solution)/shard_map/ppermute | solution.py:17
  29.1 8.4 %collective-permute-start.2 = (f32[2,70,1,256]{3,1,2,0:T(8,128)S(1)}, f32[2,70,1,256]{3,1,2,0:T(8,128)S(1)}, u32[]{:S(2)}, u32[]{:S(2)}) collective-permute-start(f32[2,70,1,256]{3,1,2,0:T(8,128)S(1)} %get-tuple-element.14), channel_id=1, source_target_pairs={{1,0},{2,1},{3,2},{4,3},{5,4},{6,5},{7,6},{9,8},{10,9},{11,10},{12... | collective-permute-start | bytes 430088 | tf_op jit(solution)/shard_map/ppermute | solution.py:18
  30.4 10.4 %collective-permute-start.3 = (f32[2,70,1,256]{3,1,2,0:T(8,128)S(1)}, f32[2,70,1,256]{3,1,2,0:T(8,128)S(1)}, u32[]{:S(2)}, u32[]{:S(2)}) collective-permute-start(f32[2,70,1,256]{3,1,2,0:T(8,128)S(1)} %get-tuple-element.15), channel_id=1, source_target_pairs={{0,1},{1,2},{2,3},{3,4},{4,5},{5,6},{6,7},{8,9},{9,10},{10,11},{11... | collective-permute-start | bytes 430088 | tf_op jit(solution)/shard_map/ppermute | solution.py:17
  42.6 8.4 %collective-permute-start.4 = (f32[2,70,1,256]{3,1,2,0:T(8,128)S(1)}, f32[2,70,1,256]{3,1,2,0:T(8,128)S(1)}, u32[]{:S(2)}, u32[]{:S(2)}) collective-permute-start(f32[2,70,1,256]{3,1,2,0:T(8,128)S(1)} %get-tuple-element.12), channel_id=1, source_target_pairs={{1,0},{2,1},{3,2},{4,3},{5,4},{6,5},{7,6},{9,8},{10,9},{11,10},{12... | collective-permute-start | bytes 430088 | tf_op jit(solution)/shard_map/ppermute | solution.py:18
  43.9 10.4 %collective-permute-start.5 = (f32[2,70,1,256]{3,1,2,0:T(8,128)S(1)}, f32[2,70,1,256]{3,1,2,0:T(8,128)S(1)}, u32[]{:S(2)}, u32[]{:S(2)}) collective-permute-start(f32[2,70,1,256]{3,1,2,0:T(8,128)S(1)} %get-tuple-element.13), channel_id=1, source_target_pairs={{0,1},{1,2},{2,3},{3,4},{4,5},{5,6},{6,7},{8,9},{9,10},{10,11},{11... | collective-permute-start | bytes 430088 | tf_op jit(solution)/shard_map/ppermute | solution.py:17
  54.3 13.5 %copy-start.2 = (bf16[2,70,16,256]{3,2,1,0:T(8,128)(2,1)S(1)}, bf16[2,70,16,256]{3,2,1,0:T(8,128)(2,1)}, u32[]{:S(2)}) copy-start(bf16[2,70,16,256]{3,2,1,0:T(8,128)(2,1)} %param.9) | copy-start | bytes 3440644
  56.1 8.4 %collective-permute-start.6 = (f32[2,70,1,256]{3,1,2,0:T(8,128)S(1)}, f32[2,70,1,256]{3,1,2,0:T(8,128)S(1)}, u32[]{:S(2)}, u32[]{:S(2)}) collective-permute-start(f32[2,70,1,256]{3,1,2,0:T(8,128)S(1)} %get-tuple-element.10), channel_id=1, source_target_pairs={{1,0},{2,1},{3,2},{4,3},{5,4},{6,5},{7,6},{9,8},{10,9},{11,10},{12... | collective-permute-start | bytes 430088 | tf_op jit(solution)/shard_map/ppermute | solution.py:18
  57.4 10.4 %collective-permute-start.7 = (f32[2,70,1,256]{3,1,2,0:T(8,128)S(1)}, f32[2,70,1,256]{3,1,2,0:T(8,128)S(1)}, u32[]{:S(2)}, u32[]{:S(2)}) collective-permute-start(f32[2,70,1,256]{3,1,2,0:T(8,128)S(1)} %get-tuple-element.11), channel_id=1, source_target_pairs={{0,1},{1,2},{2,3},{3,4},{4,5},{5,6},{6,7},{8,9},{9,10},{10,11},{11... | collective-permute-start | bytes 430088 | tf_op jit(solution)/shard_map/ppermute | solution.py:17
  67.8 4.6 %copy-start.3 = (f32[70,16,256]{2,1,0:T(8,128)S(1)}, f32[70,16,256]{2,1,0:T(8,128)}, u32[]{:S(2)}) copy-start(f32[70,16,256]{2,1,0:T(8,128)} %param.7) | copy-start | bytes 3440644
  71.6 38.7 %copy-start = (f32[70,16,256]{2,1,0:T(8,128)S(1)}, f32[70,16,256]{2,1,0:T(8,128)}, u32[]{:S(2)}) copy-start(f32[70,16,256]{2,1,0:T(8,128)} %param.6) | copy-start | bytes 3440644
Sparse Core Ops, SparseCore 0:
  71.8 38.5 all-reduce.6
where the time goes:
time: 211 us; the launch traced here: 210 us
  blocking collectives  81.1 us (38%)
  waiting for transfers between devices  57.2 us (27%)
  starting transfers between devices  26.4 us (13%)
  other arithmetic  19.4 us (9%)
  between operations  16.9 us (8%)
  local copies, waits for them, and re-layouts  5.91 us (3%)
  matrix products  3.43 us (2%)
    psum x1, blocking collectives, lanczos_sums(): squares = lax.psum(jnp.sum(residual * residual), ('mem', 'tile'))  41.4 us
    psum x1, blocking collectives, lanczos_sums(): lax.psum((jnp.sum(incr_part * image_part), jnp.sum(incr_part * incr_part)...  39.7 us
    psum x1, waiting for transfers between devices, per_device(): summed = lax.psum(partial_value, 'mem')  36.2 us
    ppermute x4, starting transfers between devices, extended(): before = lax.ppermute(last, axis, up)  21.2 us
    ppermute x4, waiting for transfers between devices, extended(): before = lax.ppermute(last, axis, up)  13.2 us
    ppermute x4, waiting for transfers between devices, extended(): after = lax.ppermute(leading, axis, down)  7.71 us
    select_n x3, other arithmetic, per_device(): jnp.where(sweep_index < step_count, localized + 0.24 * laplace, localized)  6.11 us
    ppermute x4, starting transfers between devices, extended(): after = lax.ppermute(leading, axis, down)  5.16 us
  transfers between devices with their start and end apart: 9, of which 9 were waited for; matrix products, arithmetic and copies ran while one was open for 1% of the time, Pallas kernels for 0%

commit v1 on v0

--- a/solution.py
+++ b/solution.py
@@ -31,7 +31,7 @@
 
 def lanczos_sums(image_part, incr_part, prev_part, beta_value):
     inc_img, inc_inc = lax.psum(
-        (jnp.sum(incr_part * image_part), jnp.sum(incr_part * incr_part)), ("mem", "tile")
+        lax.psum((jnp.sum(incr_part * image_part), jnp.sum(incr_part * incr_part)), "tile"), "mem"
     )
     alpha_value = inc_img / inc_inc
     residual = image_part - alpha_value * incr_part - beta_value * prev_part

time: 211 us -> 196 us (0.929)
  blocking collectives: 81.1 us -> 65.5 us
    psum x1, blocking collectives: 39.7 us -> 22 us  [lanczos_sums(): lax.psum((jnp.sum(incr_part * image_part), jnp.sum(incr_part * incr_part)...]
    psum x0 -> x1, blocking collectives: none -> 6.28 us  [lanczos_sums(): lax.psum(lax.psum((jnp.sum(incr_part * image_part), jnp.sum(incr_part * i...]
    psum x1, blocking collectives: 41.4 us -> 37.2 us  [lanczos_sums(): squares = lax.psum(jnp.sum(residual * residual), ('mem', 'tile'))]
where the time goes in v1:
time: 196 us; the launch traced here: 195 us
  blocking collectives  65.5 us (33%)
  waiting for transfers between devices  57.2 us (29%)
  starting transfers between devices  26.4 us (13%)
  other arithmetic  19.4 us (10%)
  between operations  16.9 us (9%)
  local copies, waits for them, and re-layouts  5.91 us (3%)
  matrix products  3.42 us (2%)
    psum x1, blocking collectives, lanczos_sums(): squares = lax.psum(jnp.sum(residual * residual), ('mem', 'tile'))  37.2 us
    psum x1, waiting for transfers between devices, per_device(): summed = lax.psum(partial_value, 'mem')  36.2 us
    psum x1, blocking collectives, lanczos_sums(): lax.psum((jnp.sum(incr_part * image_part), jnp.sum(incr_part * incr_part)...  22 us
    ppermute x4, starting transfers between devices, extended(): before = lax.ppermute(last, axis, up)  21.2 us
    ppermute x4, waiting for transfers between devices, extended(): before = lax.ppermute(last, axis, up)  13.2 us
    ppermute x4, waiting for transfers between devices, extended(): after = lax.ppermute(leading, axis, down)  7.72 us
    psum x1, blocking collectives, lanczos_sums(): lax.psum(lax.psum((jnp.sum(incr_part * image_part), jnp.sum(incr_part * i...  6.28 us
    select_n x3, other arithmetic, per_device(): jnp.where(sweep_index < step_count, localized + 0.24 * laplace, localized)  6.11 us
  transfers between devices with their start and end apart: 9, of which 9 were waited for; matrix products, arithmetic and copies ran while one was open for 1% of the time, Pallas kernels for 0%

profile of v1, /device:TPU:0, one launch (start us, length us, event | category | flops | bytes accessed | tf_op | source)
XLA Modules:
  0.0 194.8 jit_solution(8323719759936395672)
XLA Ops:
  7.2 2.0 %copy.20 = f32[70,16,256]{2,0,1:T(8,128)S(1)} copy(f32[70,16,256]{2,1,0:T(8,128)} %param.6) | data formatting | bytes 2293760 | tf_op args[0]
  9.9 3.4 %fusion.22 = f32[2,70,16,256]{3,1,2,0:T(8,128)S(1)} fusion(f32[70,16,256]{2,0,1:T(8,128)S(1)} %copy.20, bf16[2,70,16,256]{3,2,1,0:T(8,128)(2,1)S(1)} %copy-done.1, f32[70]{0:T(128)S(1)} %convert_element_type.17, s32[70]{0:T(128)} %param.10), kind=kOutput, calls=%fused_computation.44 | convolution fusion | flops 482885472 | bytes 4588080 | tf_op jit(solution)/shard_map/ij,mjyx->miyx/dot_general | solution.py:55
  14.1 1.3 collective-permute-start
  15.4 6.2 %collective-permute-start.1 = (f32[2,70,1,256]{3,1,2,0:T(8,128)}, f32[2,70,1,256]{3,1,2,0:T(8,128)}, u32[]{:S(2)}, u32[]{:S(2)}) collective-permute-start(f32[2,70,1,256]{3,1,2,0:T(8,128)} %get-tuple-element.19), channel_id=1, source_target_pairs={{0,1},{1,2},{2,3},{3,4},{4,5},{5,6},{6,7},{8,9},{9,10},{10,11},{11... | collective-permute-start | bytes 430088 | tf_op jit(solution)/shard_map/ppermute | solution.py:17
  21.6 1.5 collective-permute-done
  23.1 3.3 %collective-permute-done.1 = f32[2,70,1,256]{3,1,2,0:T(8,128)} collective-permute-done((f32[2,70,1,256]{3,1,2,0:T(8,128)}, f32[2,70,1,256]{3,1,2,0:T(8,128)}, u32[]{:S(2)}, u32[]{:S(2)}) %collective-permute-start.1) | collective-permute-done | bytes 143392 | tf_op jit(solution)/shard_map/ppermute | solution.py:17
  26.4 2.6 %add_select_fusion.3 = f32[2,70,16,256]{3,1,2,0:T(8,128)S(1)} fusion(f32[2,70,16,256]{3,1,2,0:T(8,128)S(1)} %fusion.22, f32[2,70,1,256]{3,1,2,0:T(8,128)} %collective-permute-done.1, f32[2,70,1,256]{3,1,2,0:T(8,128)} %collective-permute-done, pred[16]{0:T(512)(128)(4,1)S(1)} %get-tuple-element.21), kind=kLoop, calls=%fused_computation.11 | loop fusion | flops 5734400 | bytes 4874256 | tf_op jit(solution)/shard_map/jit(_where)/select_n | solution.py:71
  29.1 1.3 collective-permute-start.2
  30.4 5.0 %collective-permute-start.3 = (f32[2,70,1,256]{3,1,2,0:T(8,128)S(1)}, f32[2,70,1,256]{3,1,2,0:T(8,128)S(1)}, u32[]{:S(2)}, u32[]{:S(2)}) collective-permute-start(f32[2,70,1,256]{3,1,2,0:T(8,128)S(1)} %get-tuple-element.17), channel_id=1, source_target_pairs={{0,1},{1,2},{2,3},{3,4},{4,5},{5,6},{6,7},{8,9},{9,10},{10,11},{11... | collective-permute-start | bytes 430088 | tf_op jit(solution)/shard_map/ppermute | solution.py:17
  35.4 2.1 %collective-permute-done.2 = f32[2,70,1,256]{3,1,2,0:T(8,128)S(1)} collective-permute-done((f32[2,70,1,256]{3,1,2,0:T(8,128)S(1)}, f32[2,70,1,256]{3,1,2,0:T(8,128)S(1)}, u32[]{:S(2)}, u32[]{:S(2)}) %collective-permute-start.2) | collective-permute-done | bytes 143392 | tf_op jit(solution)/shard_map/ppermute | solution.py:18
  37.5 3.3 %collective-permute-done.3 = f32[2,70,1,256]{3,1,2,0:T(8,128)S(1)} collective-permute-done((f32[2,70,1,256]{3,1,2,0:T(8,128)S(1)}, f32[2,70,1,256]{3,1,2,0:T(8,128)S(1)}, u32[]{:S(2)}, u32[]{:S(2)}) %collective-permute-start.3) | collective-permute-done | bytes 143392 | tf_op jit(solution)/shard_map/ppermute | solution.py:17
  40.8 1.8 add_select_fusion.2
  42.6 1.3 collective-permute-start.4
  43.9 5.0 %collective-permute-start.5 = (f32[2,70,1,256]{3,1,2,0:T(8,128)S(1)}, f32[2,70,1,256]{3,1,2,0:T(8,128)S(1)}, u32[]{:S(2)}, u32[]{:S(2)}) collective-permute-start(f32[2,70,1,256]{3,1,2,0:T(8,128)S(1)} %get-tuple-element.15), channel_id=1, source_target_pairs={{0,1},{1,2},{2,3},{3,4},{4,5},{5,6},{6,7},{8,9},{9,10},{10,11},{11... | collective-permute-start | bytes 430088 | tf_op jit(solution)/shard_map/ppermute | solution.py:17
  48.9 2.1 %collective-permute-done.4 = f32[2,70,1,256]{3,1,2,0:T(8,128)S(1)} collective-permute-done((f32[2,70,1,256]{3,1,2,0:T(8,128)S(1)}, f32[2,70,1,256]{3,1,2,0:T(8,128)S(1)}, u32[]{:S(2)}, u32[]{:S(2)}) %collective-permute-start.4) | collective-permute-done | bytes 143392 | tf_op jit(solution)/shard_map/ppermute | solution.py:18
  51.0 3.3 %collective-permute-done.5 = f32[2,70,1,256]{3,1,2,0:T(8,128)S(1)} collective-permute-done((f32[2,70,1,256]{3,1,2,0:T(8,128)S(1)}, f32[2,70,1,256]{3,1,2,0:T(8,128)S(1)}, u32[]{:S(2)}, u32[]{:S(2)}) %collective-permute-start.5) | collective-permute-done | bytes 143392 | tf_op jit(solution)/shard_map/ppermute | solution.py:17
  54.3 1.7 add_select_fusion.1
  56.1 1.3 collective-permute-start.6
  57.4 5.0 %collective-permute-start.7 = (f32[2,70,1,256]{3,1,2,0:T(8,128)S(1)}, f32[2,70,1,256]{3,1,2,0:T(8,128)S(1)}, u32[]{:S(2)}, u32[]{:S(2)}) collective-permute-start(f32[2,70,1,256]{3,1,2,0:T(8,128)S(1)} %get-tuple-element.13), channel_id=1, source_target_pairs={{0,1},{1,2},{2,3},{3,4},{4,5},{5,6},{6,7},{8,9},{9,10},{10,11},{11... | collective-permute-start | bytes 430088 | tf_op jit(solution)/shard_map/ppermute | solution.py:17
  62.4 2.1 %collective-permute-done.6 = f32[2,70,1,256]{3,1,2,0:T(8,128)S(1)} collective-permute-done((f32[2,70,1,256]{3,1,2,0:T(8,128)S(1)}, f32[2,70,1,256]{3,1,2,0:T(8,128)S(1)}, u32[]{:S(2)}, u32[]{:S(2)}) %collective-permute-start.6) | collective-permute-done | bytes 143392 | tf_op jit(solution)/shard_map/ppermute | solution.py:18
  64.5 3.3 %collective-permute-done.7 = f32[2,70,1,256]{3,1,2,0:T(8,128)S(1)} collective-permute-done((f32[2,70,1,256]{3,1,2,0:T(8,128)S(1)}, f32[2,70,1,256]{3,1,2,0:T(8,128)S(1)}, u32[]{:S(2)}, u32[]{:S(2)}) %collective-permute-start.7) | collective-permute-done | bytes 143392 | tf_op jit(solution)/shard_map/ppermute | solution.py:17
  67.8 3.8 %fusion.1 = f32[70,16,256]{2,0,1:T(8,128)} fusion(f32[2,70,16,256]{3,1,2,0:T(8,128)S(1)} %add_select_fusion.1, f32[2,70,1,256]{3,1,2,0:T(8,128)S(1)} %collective-permute-done.7, f32[2,70,1,256]{3,1,2,0:T(8,128)S(1)} %collective-permute-done.6, pred[16]{0:T(512)(128)(4,1)S(1)} %get-tuple-element.20, bf16[2,70,16,256]{3,2,1,0:T(8,128)(2,1)S(1)} %copy-done.2), kind=kLoop, calls=%fused_computation.15 | loop fusion | flops 7168000 | bytes 4874256 | tf_op jit(solution)/shard_map/reduce_sum | solution.py:72
  72.4 1.7 copy.23
  74.1 36.2 %all-reduce.8.cloned.1.call-done = f32[70,16,256]{2,0,1:T(8,128)} async-done(((f32[70,16,256]{2,0,1:T(8,128)}), f32[70,16,256]{2,0,1:T(8,128)}) %all-reduce.8.cloned.1.call-update) | async-done | bytes 1146896 | tf_op jit(solution)/shard_map/psum | solution.py:80
  110.3 2.0 %multiply_add_fusion = f32[70,16,256]{2,0,1:T(8,128)S(1)} fusion(f32[70,16,256]{2,0,1:T(8,128)} %all-reduce.8.cloned.1.call-done, f32[70,16,256]{2,1,0:T(8,128)S(1)} %copy-done), kind=kLoop, calls=%fused_computation.46 | loop fusion | flops 573440 | bytes 3440640 | tf_op jit(solution)/shard_map/add | solution.py:81
  112.3 1.0 multiply_reduce_fusion.1
  113.3 22.0 %all-reduce.4 = (f32[]{:T(128)}, f32[]{:T(128)}) all-reduce(f32[]{:T(128)} %get-tuple-element.7, f32[]{:T(128)} %get-tuple-element.6), channel_id=1, replica_groups=mesh['mem'=4,'tile'=8] {'tile'}, use_global_device_ids=true, to_apply=%region_4.5 | all-reduce | flops 2 | bytes 16 | tf_op jit(solution)/shard_map/psum | solution.py:34
  135.4 6.3 %all-reduce.5 = (f32[]{:T(128)}, f32[]{:T(128)}) all-reduce(f32[]{:T(128)} %get-tuple-element.8, f32[]{:T(128)} %get-tuple-element.9), channel_id=1, replica_groups=mesh['mem'=4,'tile'=8] {'mem'}, use_global_device_ids=true, to_apply=%region_5.6 | all-reduce | flops 2 | bytes 16 | tf_op jit(solution)/shard_map/psum | solution.py:33
  143.0 2.2 %multiply_reduce_fusion = f32[]{:T(128)} fusion(f32[70,16,256]{2,0,1:T(8,128)} %copy.23, s32[]{:T(128)S(6)} %select_n.37, f32[70,16,256]{2,0,1:T(8,128)S(1)} %multiply_add_fusion, f32[70,16,256]{2,0,1:T(8,128)S(1)} %copy.20, f32[]{:T(128)} %bitcast.11, f32[]{:T(128)} %div.32), kind=kLoop, calls=%fused_computation.49 | loop fusion | flops 430079 | bytes 860176 | tf_op jit(solution)/shard_map/reduce_sum | solution.py:38
  145.2 37.2 %psum.47 = f32[]{:T(128)} all-reduce(f32[]{:T(128)} %multiply_reduce_fusion), channel_id=1, replica_groups=mesh['mem'=4,'tile'=8] {'mem','tile'}, use_global_device_ids=true, to_apply=%region_10.11 | all-reduce | flops 1 | bytes 8 | tf_op jit(solution)/shard_map/psum | solution.py:38
  183.1 3.0 %subtract_divide_fusion = f32[70,16,256]{2,0,1:T(8,128)S(1)} fusion(f32[]{:T(128)} %sqrt.3, f32[]{:T(128)} %bitcast.10, f32[]{:T(128)} %div.32, f32[70,16,256]{2,1,0:T(8,128)} %param.7, f32[70,16,256]{2,1,0:T(8,128)S(1)} %copy-done, f32[70,16,256]{2,0,1:T(8,128)} %all-reduce.8.cloned.1.call-done), kind=kLoop, calls=%fused_computation.45 | loop fusion | flops 2007040 | bytes 4587532 | tf_op jit(solution)/shard_map/div | solution.py:86
  186.1 1.4 copy.25
  (21 shorter events, 2.2 us)
Async XLA Ops:
  7.2 103.2 %all-reduce.8.cloned.1.call-start = ((), (), s32[]{:S(2)}) async-start(), calls=%async_computation | async-start | bytes 2359296 | tf_op jit(solution)/shard_map/psum | solution.py:80
  7.2 2.7 %copy-start.1 = (bf16[2,70,16,256]{3,2,1,0:T(8,128)(2,1)S(1)}, bf16[2,70,16,256]{3,2,1,0:T(8,128)(2,1)}, u32[]{:S(2)}) copy-start(bf16[2,70,16,256]{3,2,1,0:T(8,128)(2,1)} %param.9) | copy-start | bytes 3440644
  9.9 11.6 %copy-start.4 = (s32[8]{0:T(128)S(1)}, s32[8]{0:T(128)}, u32[]{:S(2)}) copy-start(s32[8]{0:T(128)} %param.11) | copy-start | bytes 100
  14.1 9.0 %collective-permute-start = (f32[2,70,1,256]{3,1,2,0:T(8,128)}, f32[2,70,1,256]{3,1,2,0:T(8,128)}, u32[]{:S(2)}, u32[]{:S(2)}) collective-permute-start(f32[2,70,1,256]{3,1,2,0:T(8,128)} %get-tuple-element.18), channel_id=1, source_target_pairs={{1,0},{2,1},{3,2},{4,3},{5,4},{6,5},{7,6},{9,8},{10,9},{11,10},{12... | collective-permute-start | bytes 430088 | tf_op jit(solution)/shard_map/ppermute | solution.py:18
  15.4 11.0 %collective-permute-start.1 = (f32[2,70,1,256]{3,1,2,0:T(8,128)}, f32[2,70,1,256]{3,1,2,0:T(8,128)}, u32[]{:S(2)}, u32[]{:S(2)}) collective-permute-start(f32[2,70,1,256]{3,1,2,0:T(8,128)} %get-tuple-element.19), channel_id=1, source_target_pairs={{0,1},{1,2},{2,3},{3,4},{4,5},{5,6},{6,7},{8,9},{9,10},{10,11},{11... | collective-permute-start | bytes 430088 | tf_op jit(solution)/shard_map/ppermute | solution.py:17
  29.1 8.4 %collective-permute-start.2 = (f32[2,70,1,256]{3,1,2,0:T(8,128)S(1)}, f32[2,70,1,256]{3,1,2,0:T(8,128)S(1)}, u32[]{:S(2)}, u32[]{:S(2)}) collective-permute-start(f32[2,70,1,256]{3,1,2,0:T(8,128)S(1)} %get-tuple-element.16), channel_id=1, source_target_pairs={{1,0},{2,1},{3,2},{4,3},{5,4},{6,5},{7,6},{9,8},{10,9},{11,10},{12... | collective-permute-start | bytes 430088 | tf_op jit(solution)/shard_map/ppermute | solution.py:18
  30.4 10.4 %collective-permute-start.3 = (f32[2,70,1,256]{3,1,2,0:T(8,128)S(1)}, f32[2,70,1,256]{3,1,2,0:T(8,128)S(1)}, u32[]{:S(2)}, u32[]{:S(2)}) collective-permute-start(f32[2,70,1,256]{3,1,2,0:T(8,128)S(1)} %get-tuple-element.17), channel_id=1, source_target_pairs={{0,1},{1,2},{2,3},{3,4},{4,5},{5,6},{6,7},{8,9},{9,10},{10,11},{11... | collective-permute-start | bytes 430088 | tf_op jit(solution)/shard_map/ppermute | solution.py:17
  42.6 8.4 %collective-permute-start.4 = (f32[2,70,1,256]{3,1,2,0:T(8,128)S(1)}, f32[2,70,1,256]{3,1,2,0:T(8,128)S(1)}, u32[]{:S(2)}, u32[]{:S(2)}) collective-permute-start(f32[2,70,1,256]{3,1,2,0:T(8,128)S(1)} %get-tuple-element.14), channel_id=1, source_target_pairs={{1,0},{2,1},{3,2},{4,3},{5,4},{6,5},{7,6},{9,8},{10,9},{11,10},{12... | collective-permute-start | bytes 430088 | tf_op jit(solution)/shard_map/ppermute | solution.py:18
  43.9 10.4 %collective-permute-start.5 = (f32[2,70,1,256]{3,1,2,0:T(8,128)S(1)}, f32[2,70,1,256]{3,1,2,0:T(8,128)S(1)}, u32[]{:S(2)}, u32[]{:S(2)}) collective-permute-start(f32[2,70,1,256]{3,1,2,0:T(8,128)S(1)} %get-tuple-element.15), channel_id=1, source_target_pairs={{0,1},{1,2},{2,3},{3,4},{4,5},{5,6},{6,7},{8,9},{9,10},{10,11},{11... | collective-permute-start | bytes 430088 | tf_op jit(solution)/shard_map/ppermute | solution.py:17
  54.3 13.5 %copy-start.2 = (bf16[2,70,16,256]{3,2,1,0:T(8,128)(2,1)S(1)}, bf16[2,70,16,256]{3,2,1,0:T(8,128)(2,1)}, u32[]{:S(2)}) copy-start(bf16[2,70,16,256]{3,2,1,0:T(8,128)(2,1)} %param.9) | copy-start | bytes 3440644
  56.1 8.4 %collective-permute-start.6 = (f32[2,70,1,256]{3,1,2,0:T(8,128)S(1)}, f32[2,70,1,256]{3,1,2,0:T(8,128)S(1)}, u32[]{:S(2)}, u32[]{:S(2)}) collective-permute-start(f32[2,70,1,256]{3,1,2,0:T(8,128)S(1)} %get-tuple-element.12), channel_id=1, source_target_pairs={{1,0},{2,1},{3,2},{4,3},{5,4},{6,5},{7,6},{9,8},{10,9},{11,10},{12... | collective-permute-start | bytes 430088 | tf_op jit(solution)/shard_map/ppermute | solution.py:18
  57.4 10.4 %collective-permute-start.7 = (f32[2,70,1,256]{3,1,2,0:T(8,128)S(1)}, f32[2,70,1,256]{3,1,2,0:T(8,128)S(1)}, u32[]{:S(2)}, u32[]{:S(2)}) collective-permute-start(f32[2,70,1,256]{3,1,2,0:T(8,128)S(1)} %get-tuple-element.13), channel_id=1, source_target_pairs={{0,1},{1,2},{2,3},{3,4},{4,5},{5,6},{6,7},{8,9},{9,10},{10,11},{11... | collective-permute-start | bytes 430088 | tf_op jit(solution)/shard_map/ppermute | solution.py:17
  67.8 4.6 %copy-start.3 = (f32[70,16,256]{2,1,0:T(8,128)S(1)}, f32[70,16,256]{2,1,0:T(8,128)}, u32[]{:S(2)}) copy-start(f32[70,16,256]{2,1,0:T(8,128)} %param.7) | copy-start | bytes 3440644
  71.6 38.7 %copy-start = (f32[70,16,256]{2,1,0:T(8,128)S(1)}, f32[70,16,256]{2,1,0:T(8,128)}, u32[]{:S(2)}) copy-start(f32[70,16,256]{2,1,0:T(8,128)} %param.6) | copy-start | bytes 3440644
Sparse Core Ops, SparseCore 0:
  71.8 38.5 all-reduce.7
